TPU v7x, 32 devices: a whole 2x2x4 slice. The times are simulated.
32 devices in a mesh: group: 2 (over x), route: 4 (over y, core), cuts: 4 (over z).
Axes of the slice: x: 2, y: 2, z: 4, core: 2. Of those that a mesh axis runs over, the one named last changes fastest.
Arguments:
- query_matrix_rows: bfloat16 [1024, 4096], P(('group', 'route'), 'cuts'), parts along dimension 0, may hold values from -8 to 8
- key_matrix_rows: bfloat16 [1024, 1024], P(('group', 'route'), 'cuts'), parts along dimension 0, may hold values from -8 to 8
- value_matrix_rows: bfloat16 [1024, 1024], P(('group', 'route'), 'cuts'), parts along dimension 0, may hold values from -6 to 6
- attention_output_matrix: bfloat16 [4096, 4096], P('cuts'), may hold values from -0.125 to 0.125
- residual: bfloat16 [1024, 4096], P(('group', 'route'), 'cuts'), parts along dimension 0, may hold values from -6 to 6
- cotangent: bfloat16 [1024, 4096], P(('group', 'route'), 'cuts'), parts along dimension 0, may hold values from -0.59765625 to 0.59765625
- token_expert_choices: int32 [1024, 2], P(('group', 'route')), parts along dimension 0, may hold values from 0 to 3, as said below
- token_slot_positions: int32 [1024, 2], P(('group', 'route')), parts along dimension 0, may hold values from 0 to 127, as said below
- router_choice_weight: float32 [1024, 2], P(('group', 'route')), parts along dimension 0, may hold values from 0.2 to 1
- expert_gate_weight: bfloat16 [4, 3200, 4096], P('route', 'cuts'), may hold values from -0.09375 to 0.09375
- expert_down_weight: bfloat16 [4, 3200, 4096], P('route', 'cuts'), may hold values from -0.15625 to 0.15625
- adapter_down_factor: bfloat16 [4, 64, 4096], P('route'), may hold values from -0.09375 to 0.09375
- adapter_up_factor: bfloat16 [4, 64, 3200], P('route', None, 'cuts'), may hold values from -0.75 to 0.75
Outputs:
- layer_out: bfloat16 [1024, 4096], P(('group', 'route'), 'cuts'), parts along dimension 0
- down_factor_gradient: float32 [8, 64, 4096], P(('group', 'route'), None, 'cuts'), parts along dimension 0
- up_factor_gradient: float32 [8, 64, 3200], P(('group', 'route'), None, 'cuts'), parts along dimension 0
There are 2 independent parts, one for each index of `group`. A program takes and returns all parts, laid end to end along the dimension named above; an argument that names none is the same for every part. Nothing has to cross between parts.
Inputs may be any that keep to these rules, and one draw needn't show every extreme that they name: `token_expert_choices`: the two experts of a token differ. Within one sequence of 128 tokens no expert is named more than 128 times; one expert, the same for all sequences of a draw, is named exactly 128 times in every sequence. `token_slot_positions`: within one sequence the slots given for one expert are all different.
All inputs are finite; a program needn't handle non-finite values.
Results may differ from a plain program's by a relative error of at most 0.014.
Values may be sent and summed in bfloat16 or wider, within the bound.
No kernel may reach another device: no remote copies, remote signals or barrier semaphores. Data moves between devices by JAX's collectives and lax.ppermute only.
A program may use at most 128 MiB of HBM per device.

v0:
```python
import math
import jax
import jax.numpy as jnp
from jax import lax
from jax.sharding import PartitionSpec as P

HEAD_DIM = 128
ADAPTER_SCALE = 0.5


def causal_heads(query_matrix_rows, key_matrix_rows, value_matrix_rows):
    length = query_matrix_rows.shape[0]
    kv_local = key_matrix_rows.shape[1] // HEAD_DIM
    per_kv = query_matrix_rows.shape[1] // key_matrix_rows.shape[1]
    queries = query_matrix_rows.reshape(length, kv_local, per_kv, HEAD_DIM)
    key_view = key_matrix_rows.reshape(length, kv_local, HEAD_DIM)
    value_view = value_matrix_rows.reshape(length, kv_local, HEAD_DIM)
    scores = jnp.einsum(
        "qhgd,khd->hgqk", queries, key_view, preferred_element_type=jnp.float32
    ) / math.sqrt(HEAD_DIM)
    future = lax.broadcasted_iota(jnp.int32, (length, length), 1) > lax.broadcasted_iota(
        jnp.int32, (length, length), 0
    )
    scores = jnp.where(future, -jnp.inf, scores)
    row_max = jnp.max(scores, axis=-1, keepdims=True)
    shifted = jnp.exp(scores - row_max)
    weights = (shifted / jnp.sum(shifted, axis=-1, keepdims=True)).astype(jnp.bfloat16)
    attended = jnp.einsum("hgqk,khd->qhgd", weights, value_view, preferred_element_type=jnp.float32)
    return attended.astype(jnp.bfloat16).reshape(length, query_matrix_rows.shape[1])


def fill_slots(source_rows, owners):
    padded = jnp.concatenate(
        [source_rows, jnp.zeros((1, source_rows.shape[1]), source_rows.dtype)], axis=0
    )
    return jnp.take(padded, owners, axis=0)


def weighted_slots(source_rows, owners, scales):
    return (fill_slots(source_rows, owners).astype(jnp.float32) * scales[:, None]).astype(
        jnp.bfloat16
    )


def combine_rows(returned, cell_ids, router_choice_weight):
    first_out = jnp.take(returned, cell_ids[:, 0], axis=0)
    second_out = jnp.take(returned, cell_ids[:, 1], axis=0)
    return router_choice_weight[:, 0:1] * first_out + router_choice_weight[:, 1:2] * second_out


def local(
    query_matrix_rows,
    key_matrix_rows,
    value_matrix_rows,
    attention_output_matrix,
    residual,
    cotangent,
    token_expert_choices,
    token_slot_positions,
    router_choice_weight,
    expert_gate_weight,
    expert_down_weight,
    adapter_down_factor,
    adapter_up_factor,
):
    attended = causal_heads(query_matrix_rows, key_matrix_rows, value_matrix_rows)
    head_terms = jnp.dot(attended, attention_output_matrix, preferred_element_type=jnp.float32)
    head_cols = lax.psum_scatter(head_terms, "cuts", scatter_dimension=1, tiled=True)
    hidden_cols = (residual.astype(jnp.float32) + head_cols).astype(jnp.bfloat16)
    length = residual.shape[0]
    col_count = residual.shape[1]
    model_width = expert_gate_weight.shape[2]
    experts = lax.axis_size("route")
    capacity = 4 * length // experts
    cell_ids = token_expert_choices * capacity + token_slot_positions
    flat_cells = cell_ids.reshape(-1)
    owners = (
        jnp.full((experts * capacity,), length, jnp.int32)
        .at[flat_cells]
        .set(jnp.repeat(jnp.arange(length, dtype=jnp.int32), 2))
    )
    scales = (
        jnp.zeros((experts * capacity,), jnp.float32)
        .at[flat_cells]
        .set(router_choice_weight.reshape(-1))
    )
    full_x, full_g = (
        lax.all_gather(hidden_cols, "cuts", axis=1, tiled=True),
        lax.all_gather(cotangent, "cuts", axis=1, tiled=True),
    )
    token_part = fill_slots(full_x, owners).reshape(experts, capacity, model_width)
    grad_part = weighted_slots(full_g, owners, scales).reshape(experts, capacity, model_width)
    slot_x, slot_g = (
        lax.all_to_all(token_part, "route", split_axis=0, concat_axis=0, tiled=True),
        lax.all_to_all(grad_part, "route", split_axis=0, concat_axis=0, tiled=True),
    )
    expert_input_rows = slot_x.reshape(-1, model_width)
    rows_g = slot_g.reshape(-1, model_width)
    reduce_final_axis = (((1,), (1,)), ((), ()))
    contract_first = (((0,), (0,)), ((), ()))
    gate_primary_product = lax.dot_general(
        expert_input_rows,
        expert_gate_weight[0],
        reduce_final_axis,
        preferred_element_type=jnp.float32,
    )
    adapter_product = lax.dot_general(
        expert_input_rows,
        adapter_down_factor[0],
        reduce_final_axis,
        preferred_element_type=jnp.float32,
    ).astype(jnp.bfloat16)
    gate_preactivation = gate_primary_product + ADAPTER_SCALE * jnp.dot(
        adapter_product, adapter_up_factor[0], preferred_element_type=jnp.float32
    )
    sigmoid_gate = jax.nn.sigmoid(gate_preactivation)
    activ = (gate_preactivation * sigmoid_gate).astype(jnp.bfloat16)
    partial_out = jnp.dot(activ, expert_down_weight[0], preferred_element_type=jnp.float32).astype(
        jnp.bfloat16
    )
    slot_sums = lax.psum_scatter(
        partial_out.astype(jnp.float32)
        .reshape(experts, capacity, model_width)
        .astype(jnp.bfloat16),
        "cuts",
        scatter_dimension=2,
        tiled=True,
    ).astype(jnp.float32)
    returned = (
        lax.all_to_all(
            slot_sums.astype(jnp.bfloat16), "route", split_axis=0, concat_axis=0, tiled=True
        )
        .astype(slot_sums.dtype)
        .reshape(experts * capacity, col_count)
    )
    merged = hidden_cols.astype(jnp.float32) + combine_rows(
        returned, cell_ids, router_choice_weight
    )
    layer_out = merged.astype(jnp.bfloat16)
    grad_hidden = lax.dot_general(
        rows_g, expert_down_weight[0], reduce_final_axis, preferred_element_type=jnp.float32
    )
    preactivation_gradient = (
        grad_hidden * sigmoid_gate * (1.0 + gate_preactivation * (1.0 - sigmoid_gate))
    ).astype(jnp.bfloat16)
    up_factor_gradient = ADAPTER_SCALE * lax.dot_general(
        adapter_product, preactivation_gradient, contract_first, preferred_element_type=jnp.float32
    )
    factor_part = lax.dot_general(
        preactivation_gradient,
        adapter_up_factor[0],
        reduce_final_axis,
        preferred_element_type=jnp.float32,
    ).astype(jnp.bfloat16)
    gradient_pieces = lax.dot_general(
        factor_part, expert_input_rows, contract_first, preferred_element_type=jnp.float32
    )
    down_factor_gradient = ADAPTER_SCALE * lax.psum_scatter(
        gradient_pieces.astype(jnp.bfloat16), "cuts", scatter_dimension=1, tiled=True
    ).astype(jnp.float32)
    return (layer_out, down_factor_gradient[None], up_factor_gradient[None])


def solution(mesh):
    return jax.shard_map(
        local,
        mesh=mesh,
        in_specs=(
            P(("group", "route"), "cuts"),
            P(("group", "route"), "cuts"),
            P(("group", "route"), "cuts"),
            P("cuts", None),
            P(("group", "route"), "cuts"),
            P(("group", "route"), "cuts"),
            P(("group", "route"), None),
            P(("group", "route"), None),
            P(("group", "route"), None),
            P("route", "cuts", None),
            P("route", "cuts", None),
            P("route", None, None),
            P("route", None, "cuts"),
        ),
        out_specs=(
            P(("group", "route"), "cuts"),
            P(("group", "route"), None, "cuts"),
            P(("group", "route"), None, "cuts"),
        ),
        check_vma=False,
    )
```

profile of v0, /device:TPU:0, one launch (start us, length us, event | category | flops | bytes accessed | tf_op | source)
XLA Modules:
  0.0 290.6 jit_solution(17472282540791643243)
XLA Ops:
  7.2 0.0 copy-start
  7.2 0.0 reduce-scatter.4.cloned.1.call-start
  7.2 1.2 reshape.89
  8.4 0.9 reshape.88
  9.3 0.2 fusion.15
  9.5 0.3 fusion.39
  9.9 1.0 copy.31
  10.8 0.3 convolution_convert_fusion.1
  11.1 0.0 copy-start.4
  11.1 0.0 copy-start.6
  11.2 0.0 copy-start.7
  11.2 6.0 %fusion.44 = f32[128,4096]{1,0:T(8,128)} fusion(bf16[128,1024]{0,1:T(8,128)(2,1)S(1)} %bitcast.77, bf16[1024,4096]{1,0:T(8,128)(2,1)} %param.20), kind=kOutput, calls=%fused_computation.69 | convolution fusion | flops 1073741824 | bytes 10747904 | tf_op jit(solution)/shard_map/dot_general | solution.py:67
  17.2 0.0 reduce-scatter.4.cloned.1.call-update
  17.2 0.0 all-gather.3.cloned.1.call-start
  17.3 46.5 %reduce-scatter.4.cloned.1.call-done = f32[128,1024]{1,0:T(8,128)} async-done(((f32[128,4096]{1,0:T(8,128)}), f32[128,1024]{1,0:T(8,128)}) %reduce-scatter.4.cloned.1.call-update) | async-done | bytes 524304 | tf_op jit(solution)/shard_map/reduce_scatter | solution.py:68
  63.7 1.8 add_convert_fusion
  65.5 0.0 all-gather.3.cloned.1.call-update
  65.6 0.0 copy-done.6
  65.6 0.0 copy-done.7
  65.6 0.1 copy.24
  65.7 0.1 reshape.92
  65.9 0.1 reshape.139
  66.0 1.4 scatter_custom_fusion
  67.4 25.6 %all-gather.3.cloned.1.call-done = bf16[128,4096]{1,0:T(8,128)(2,1)} async-done(((bf16[128,1024]{1,0:T(8,128)(2,1)}), bf16[128,4096]{1,0:T(8,128)(2,1)}) %all-gather.3.cloned.1.call-update) | async-done | bytes 1048592 | tf_op jit(solution)/shard_map/all_gather | solution.py:88
  93.1 1.3 concatenate.6
  94.4 4.4 %gather_fusion = bf16[512,4096]{1,0:T(8,128)(2,1)} fusion(bf16[129,4096]{1,0:T(8,128)(2,1)S(1)} %concatenate.6, s32[1024]{0:T(1024)S(1)} %pad_clamp_fusion.2), kind=kCustom, calls=%fused_computation.clone | custom fusion | bytes 8390656 | tf_op jit(solution)/shard_map/jit(_take)/gather | solution.py:36
  98.8 4.6 %broadcast_select_fusion = bf16[512,4096]{1,0:T(8,128)(2,1)} fusion(bf16[512,4096]{1,0:T(8,128)(2,1)} %gather_fusion, pred[512]{0:T(512)(128)(4,1)S(1)} %compare_and_fusion.2), kind=kLoop, calls=%fused_computation.16 | loop fusion | flops 2097152 | bytes 8389120 | tf_op jit(solution)/shard_map/jit(_take)/select_n | solution.py:36
  103.4 4.8 %all-to-all-start = ((bf16[4,128,4096]{2,1,0:T(8,128)(2,1)}), bf16[4,128,4096]{2,1,0:T(8,128)(2,1)}, u32[]{:S(2)}, u32[]{:S(2)}) async-start(bf16[4,128,4096]{2,1,0:T(8,128)(2,1)} %bitcast.74), calls=%async_computation.1 | async-start | bytes 8388608 | tf_op jit(solution)/shard_map/all_to_all | solution.py:94
  108.3 0.0 all-gather.5.cloned.1.call-start
  108.3 0.7 all-gather.5.cloned.1.call-update
  109.0 0.0 reduce-scatter.6.cloned.1.call-start
  109.0 47.4 %all-to-all-done = bf16[4,128,4096]{2,1,0:T(8,128)(2,1)} async-done(((bf16[4,128,4096]{2,1,0:T(8,128)(2,1)}), bf16[4,128,4096]{2,1,0:T(8,128)(2,1)}, u32[]{:S(2)}, u32[]{:S(2)}) %all-to-all-start) | async-done | bytes 4194336 | tf_op jit(solution)/shard_map/all_to_all | solution.py:94
  156.5 7.0 %fusion.5 = f32[512,800]{0,1:T(8,128)S(1)} fusion(bf16[512,4096]{1,0:T(8,128)(2,1)} %bitcast.11, bf16[1,800,4096]{2,1,0:T(8,128)(2,1)} %param.26), kind=kOutput, calls=%fused_computation.12 | convolution fusion | flops 3355443200 | bytes 12386304 | tf_op jit(solution)/shard_map/dot_general | solution.py:101
  163.5 0.0 copy-start.3
  163.5 3.6 %convolution_convert_fusion.3 = bf16[512,64]{0,1:T(8,128)(2,1)S(1)} fusion(bf16[512,4096]{1,0:T(8,128)(2,1)} %bitcast.11, bf16[1,64,4096]{2,1,0:T(8,128)(2,1)S(1)} %copy-done), kind=kOutput, calls=%fused_computation.30 | convolution fusion | flops 268468224 | bytes 4784128 | tf_op jit(solution)/shard_map/dot_general | solution.py:107
  167.1 0.4 multiply_add_fusion
  167.5 9.1 %fusion.7 = bf16[512,4096]{1,0:T(8,128)(2,1)} fusion(bf16[1,800,4096]{2,1,0:T(8,128)(2,1)} %param.27, f32[512,800]{0,1:T(8,128)S(1)} %multiply_add_fusion), kind=kOutput, calls=%fused_computation.14 | convolution fusion | flops 3359588352 | bytes 12386304 | tf_op jit(solution)/shard_map/dot_general | solution.py:118
  176.7 0.0 reduce-scatter.6.cloned.1.call-update
  176.7 0.2 reduce-scatter.8.cloned.1.call-start
  176.9 0.4 copy-done.5
  177.3 0.1 copy.25
  177.4 0.1 reshape.147
  177.6 1.4 scatter_custom_fusion.1
  179.0 0.0 all-gather.5.cloned.1.call-done
  179.0 1.3 concatenate.7
  180.4 4.4 %gather_fusion.3 = bf16[512,4096]{1,0:T(8,128)(2,1)} fusion(bf16[129,4096]{1,0:T(8,128)(2,1)S(1)} %concatenate.7, s32[1024]{0:T(1024)S(1)} %pad_clamp_fusion.2), kind=kCustom, calls=%fused_computation.2.clone | custom fusion | bytes 8390656 | tf_op jit(solution)/shard_map/jit(_take)/gather | solution.py:36
  184.7 4.7 %multiply_convert_fusion = bf16[512,4096]{1,0:T(8,128)(2,1)S(1)} fusion(bf16[512,4096]{1,0:T(8,128)(2,1)} %gather_fusion.3, f32[512]{0:T(512)S(1)} %scatter_custom_fusion.1, pred[512]{0:T(512)(128)(4,1)S(1)} %compare_and_fusion.2), kind=kLoop, calls=%fused_computation.7 | loop fusion | flops 8388608 | bytes 8391168 | tf_op jit(solution)/shard_map/convert_element_type | solution.py:40
  189.5 0.0 slice-start.1
  189.5 50.8 %all_to_all.15 = bf16[4,128,4096]{2,1,0:T(8,128)(2,1)S(1)} all-to-all(bf16[4,128,4096]{2,1,0:T(8,128)(2,1)S(1)} %bitcast.73), channel_id=1, replica_groups=mesh['group'=2,'route'=4,'cuts'=4] {'route'}, dimensions={0} | all-to-all | bytes 8388608 | tf_op jit(solution)/shard_map/all_to_all | solution.py:95
  240.3 3.9 %multiply_convert_fusion.1 = bf16[512,800]{0,1:T(8,128)(2,1)S(1)} fusion(f32[512,800]{0,1:T(8,128)S(1)} %multiply_add_fusion, bf16[512,4096]{1,0:T(8,128)(2,1)S(1)} %bitcast.76, bf16[1,800,4096]{2,1,0:T(8,128)(2,1)S(1)} %bitcast.84), kind=kOutput, calls=%fused_computation.17 | convolution fusion | flops 3359129600 | bytes 13205504 | tf_op jit(solution)/shard_map/dot_general | solution.py:140
  244.3 4.6 %convolution_convert_fusion = bf16[64,4096]{1,0:T(8,128)(2,1)} fusion(bf16[512,4096]{1,0:T(8,128)(2,1)} %bitcast.11, bf16[512,800]{0,1:T(8,128)(2,1)S(1)} %multiply_convert_fusion.1, bf16[1,64,800]{2,1,0:T(8,128)(2,1)S(1)} %copy-done.3), kind=kOutput, calls=%fused_computation.15 | convolution fusion | flops 321159168 | bytes 5640192 | tf_op jit(solution)/shard_map/dot_general | solution.py:155
  248.9 0.0 reduce-scatter.8.cloned.1.call-update
  248.9 3.2 %reduce-scatter.6.cloned.1.call-done = bf16[4,128,1024]{2,1,0:T(8,128)(2,1)} async-done(((bf16[4,128,4096]{2,1,0:T(8,128)(2,1)}), bf16[4,128,1024]{2,1,0:T(8,128)(2,1)}) %reduce-scatter.6.cloned.1.call-update) | async-done | bytes 1048592 | tf_op jit(solution)/shard_map/reduce_scatter | solution.py:121
  252.1 4.2 %all-to-all-start.1 = ((bf16[4,128,1024]{2,1,0:T(8,128)(2,1)}), bf16[4,128,1024]{2,1,0:T(8,128)(2,1)}, u32[]{:S(2)}, u32[]{:S(2)}) async-start(bf16[4,128,1024]{2,1,0:T(8,128)(2,1)} %reduce-scatter.6.cloned.1.call-done), calls=%async_computation.3 | async-start | bytes 2097152 | tf_op jit(solution)/shard_map/all_to_all | solution.py:130
  256.4 1.1 fusion.16
  257.5 19.1 %reduce-scatter.8.cloned.1.call-done = bf16[64,1024]{1,0:T(8,128)(2,1)} async-done(((bf16[64,4096]{1,0:T(8,128)(2,1)}), bf16[64,1024]{1,0:T(8,128)(2,1)}) %reduce-scatter.8.cloned.1.call-update) | async-done | bytes 131088 | tf_op jit(solution)/shard_map/reduce_scatter | solution.py:158
  276.6 1.6 multiply_bitcast_fusion
  278.2 0.0 all-to-all-done.1
  278.2 1.5 bitcast_convert_fusion
  279.7 0.0 copy-start.2
  279.7 0.0 copy-start.1
  279.7 0.8 gather_fusion.1
  280.5 1.6 gather_fusion.2
  282.1 2.0 fusion.21
  (20 shorter events, 0.1 us)
Async XLA Ops:
  7.2 156.3 %copy-start = (bf16[1,64,4096]{2,1,0:T(8,128)(2,1)S(1)}, bf16[1,64,4096]{2,1,0:T(8,128)(2,1)}, u32[]{:S(2)}) copy-start(bf16[1,64,4096]{2,1,0:T(8,128)(2,1)} %param.28) | copy-start | bytes 1572868
  7.2 56.5 %reduce-scatter.4.cloned.1.call-start = ((), (), s32[]{:S(2)}) async-start(), calls=%async_computation.6 | async-start | bytes 2621440 | tf_op jit(solution)/shard_map/reduce_scatter | solution.py:68
  11.1 52.6 %copy-start.4 = (bf16[128,1024]{1,0:T(8,128)(2,1)S(1)}, bf16[128,1024]{1,0:T(8,128)(2,1)}, u32[]{:S(2)}) copy-start(bf16[128,1024]{1,0:T(8,128)(2,1)} %param.21) | copy-start | bytes 786436
  11.1 54.4 %copy-start.6 = (s32[128,2]{0,1:T(2,128)S(1)}, s32[128,2]{0,1:T(2,128)}, u32[]{:S(2)}) copy-start(s32[128,2]{0,1:T(2,128)} %param.24) | copy-start | bytes 3076
  11.2 54.4 %copy-start.7 = (s32[128,2]{0,1:T(2,128)S(1)}, s32[128,2]{0,1:T(2,128)}, u32[]{:S(2)}) copy-start(s32[128,2]{0,1:T(2,128)} %param.23) | copy-start | bytes 3076
  17.2 75.9 %all-gather.3.cloned.1.call-start = ((), (), s32[]{:S(2)}) async-start(), calls=%async_computation.7 | async-start | bytes 1310720 | tf_op jit(solution)/shard_map/all_gather | solution.py:88
  103.4 53.0 %all-to-all-start = ((bf16[4,128,4096]{2,1,0:T(8,128)(2,1)}), bf16[4,128,4096]{2,1,0:T(8,128)(2,1)}, u32[]{:S(2)}, u32[]{:S(2)}) async-start(bf16[4,128,4096]{2,1,0:T(8,128)(2,1)} %bitcast.74), calls=%async_computation.1 | async-start | bytes 8388608 | tf_op jit(solution)/shard_map/all_to_all | solution.py:94
  108.3 70.8 %all-gather.5.cloned.1.call-start = ((), (), s32[]{:S(2)}) async-start(), calls=%async_computation.9 | async-start | bytes 1310720 | tf_op jit(solution)/shard_map/all_gather | solution.py:89
  109.0 143.1 %reduce-scatter.6.cloned.1.call-start = ((), (), s32[]{:S(2)}) async-start(), calls=%async_computation.8 | async-start | bytes 5242880 | tf_op jit(solution)/shard_map/reduce_scatter | solution.py:121
  163.5 3.6 %copy-start.3 = (bf16[1,64,800]{2,1,0:T(8,128)(2,1)S(1)}, bf16[1,64,800]{2,1,0:T(8,128)(2,1)}, u32[]{:S(2)}) copy-start(bf16[1,64,800]{2,1,0:T(8,128)(2,1)} %param.29) | copy-start | bytes 307204
  176.7 0.7 copy-start.5
  176.7 99.9 %reduce-scatter.8.cloned.1.call-start = ((), (), s32[]{:S(2)}) async-start(), calls=%async_computation.10 | async-start | bytes 655360 | tf_op jit(solution)/shard_map/reduce_scatter | solution.py:158
  184.7 55.6 %slice-start = ((s8[6553600]{0:T(1024)(128)(4,1)}), s8[4194304]{0:T(1024)(128)(4,1)S(1)}, s32[]{:S(2)}) async-start(s8[6553600]{0:T(1024)(128)(4,1)} %bitcast.83), calls=%async_computation.11 | async-start | bytes 8388608
  189.5 50.9 %slice-start.1 = ((s8[6553600]{0:T(1024)(128)(4,1)}), s8[2359296]{0:T(1024)(128)(4,1)S(1)}, s32[]{:S(2)}) async-start(s8[6553600]{0:T(1024)(128)(4,1)} %bitcast.83), calls=%async_computation.12 | async-start | bytes 4718592
  252.1 26.1 %all-to-all-start.1 = ((bf16[4,128,1024]{2,1,0:T(8,128)(2,1)}), bf16[4,128,1024]{2,1,0:T(8,128)(2,1)}, u32[]{:S(2)}, u32[]{:S(2)}) async-start(bf16[4,128,1024]{2,1,0:T(8,128)(2,1)} %reduce-scatter.6.cloned.1.call-done), calls=%async_computation.3 | async-start | bytes 2097152 | tf_op jit(solution)/shard_map/all_to_all | solution.py:130
  279.7 2.4 copy-start.2
  279.7 4.4 %copy-start.1 = (bf16[1,64,4096]{2,1,0:T(8,128)(2,1)S(1)}, bf16[1,64,4096]{2,1,0:T(8,128)(2,1)}, u32[]{:S(2)}) copy-start(bf16[1,64,4096]{2,1,0:T(8,128)(2,1)} %param.28) | copy-start | bytes 1572868
Sparse Core Ops, SparseCore 0:
  17.3 46.3 reduce-scatter.3
  65.9 27.1 all-gather.2
  110.6 27.8 all-gather.4
  176.8 75.2 reduce-scatter.5
  254.2 22.3 reduce-scatter.7
where the time goes:
time: 291 us
  waiting for transfers between devices  143 us (49%)
  blocking collectives  50.8 us (17%)
  matrix products  36.7 us (13%)
  local copies, waits for them, and re-layouts  20.7 us (7%)
  other arithmetic  16.2 us (6%)
  between operations  14.1 us (5%)
  starting transfers between devices  9.47 us (3%)
    all_to_all x1, blocking collectives, local(): lax.all_to_all(grad_part, 'route', split_axis=0, concat_axis=0, tiled=True)  50.8 us
    all_to_all x1, waiting for transfers between devices, local(): lax.all_to_all(token_part, 'route', split_axis=0, concat_axis=0, tiled=True)  47.4 us
    reduce_scatter x1, waiting for transfers between devices, local(): lax.psum_scatter(head_terms, 'cuts', scatter_dimension=1, tiled=True)  46.5 us
    all_gather x1, waiting for transfers between devices, local(): lax.all_gather(hidden_cols, 'cuts', axis=1, tiled=True)  25.6 us
    reduce_scatter x1, waiting for transfers between devices, local(): lax.psum_scatter(gradient_pieces.astype(jnp.bfloat16), 'cuts', scatter_di...  19.1 us
    dot_general x1, matrix products, local(): jnp.dot(activ, expert_down_weight[0], preferred_element_type=jnp.float32)  9.11 us
    gather x2, local copies, waits for them, and re-layouts, fill_slots(): return jnp.take(padded, owners, axis=0)  8.77 us
    dot_general x1, matrix products, local(): lax.dot_general(expert_input_rows, expert_gate_weight[0], reduce_final_ax...  7 us
  transfers between devices with their start and end apart: 7, of which 5 were waited for; matrix products, arithmetic and copies ran while one was open for 16% of the time, Pallas kernels for 0%

commit v1 on v0

--- a/solution.py
+++ b/solution.py
@@ -6,6 +6,18 @@
 
 HEAD_DIM = 128
 ADAPTER_SCALE = 0.5
+
+
+def collect(value, axis, dim):
+    ways, here = (lax.axis_size(axis), lax.axis_index(axis))
+    grown, reach = (value, 1)
+    while reach < ways:
+        theirs = lax.ppermute(grown, axis, [(d, d ^ reach) for d in range(ways)])
+        mine_first = jnp.concatenate([grown, theirs], axis=dim)
+        theirs_first = jnp.concatenate([theirs, grown], axis=dim)
+        grown = jnp.where(here & reach == 0, mine_first, theirs_first)
+        reach = 2 * reach
+    return grown
 
 
 def causal_heads(query_matrix_rows, key_matrix_rows, value_matrix_rows):
@@ -85,7 +97,7 @@
         .set(router_choice_weight.reshape(-1))
     )
     full_x, full_g = (
-        lax.all_gather(hidden_cols, "cuts", axis=1, tiled=True),
+        collect(hidden_cols, "cuts", 1),
         lax.all_gather(cotangent, "cuts", axis=1, tiled=True),
     )
     token_part = fill_slots(full_x, owners).reshape(experts, capacity, model_width)

time: 291 us -> 296 us (1.017)
  matrix products: 36.7 us -> 40.3 us
    ppermute x0 -> x2, waiting for transfers between devices: none -> 27.7 us  [collect(): theirs = lax.ppermute(grown, axis, [(d, d ^ reach) for d in range(ways)])]
    all_gather x1 -> x0, waiting for transfers between devices: 25.6 us -> none  [local(): lax.all_gather(hidden_cols, 'cuts', axis=1, tiled=True)]
    dot_general x1, matrix products: 3.93 us -> 7 us  [local(): lax.dot_general(rows_g, expert_down_weight[0], reduce_final_axis, preferr...]
  transfers between devices with their start and end apart: 7 -> 8, of which waited for: 5 -> 6; matrix products, arithmetic and copies ran while one was open for 16% -> 17% of each run, Pallas kernels for 0% -> 0%
where the time goes in v1:
time: 296 us; the launch traced here: 295 us
  waiting for transfers between devices  142 us (48%)
  blocking collectives  50.8 us (17%)
  matrix products  40.3 us (14%)
  local copies, waits for them, and re-layouts  19.5 us (7%)
  other arithmetic  15.8 us (5%)
  between operations  14.1 us (5%)
  starting transfers between devices  12.2 us (4%)
    all_to_all x1, blocking collectives, local(): lax.all_to_all(grad_part, 'route', split_axis=0, concat_axis=0, tiled=True)  50.8 us
    all_to_all x1, waiting for transfers between devices, local(): lax.all_to_all(token_part, 'route', split_axis=0, concat_axis=0, tiled=True)  47.4 us
    reduce_scatter x1, waiting for transfers between devices, local(): lax.psum_scatter(head_terms, 'cuts', scatter_dimension=1, tiled=True)  46.5 us
    ppermute x2, waiting for transfers between devices, collect(): theirs = lax.ppermute(grown, axis, [(d, d ^ reach) for d in range(ways)])  27.7 us
    reduce_scatter x1, waiting for transfers between devices, local(): lax.psum_scatter(gradient_pieces.astype(jnp.bfloat16), 'cuts', scatter_di...  19.1 us
    dot_general x1, matrix products, local(): jnp.dot(activ, expert_down_weight[0], preferred_element_type=jnp.float32)  9.71 us
    gather x2, local copies, waits for them, and re-layouts, fill_slots(): return jnp.take(padded, owners, axis=0)  8.8 us
    dot_general x1, matrix products, local(): lax.dot_general(expert_input_rows, expert_gate_weight[0], reduce_final_ax...  7 us
  transfers between devices with their start and end apart: 8, of which 6 were waited for; matrix products, arithmetic and copies ran while one was open for 17% of the time, Pallas kernels for 0%

profile of v1, /device:TPU:0, one launch (start us, length us, event | category | flops | bytes accessed | tf_op | source)
XLA Modules:
  0.0 294.8 jit_solution(2137883800978571989)
XLA Ops:
  7.2 0.0 copy-start
  7.2 0.0 reduce-scatter.4.cloned.1.call-start
  7.2 1.2 reshape.89
  8.4 0.9 reshape.88
  9.3 0.3 fusion.39
  9.6 0.2 fusion.15
  9.9 1.0 copy.31
  10.8 0.3 convolution_convert_fusion.1
  11.1 0.0 copy-start.5
  11.1 0.0 copy-start.7
  11.1 0.0 copy-start.8
  11.2 6.0 %fusion.44 = f32[128,4096]{1,0:T(8,128)} fusion(bf16[128,1024]{0,1:T(8,128)(2,1)S(1)} %bitcast.77, bf16[1024,4096]{1,0:T(8,128)(2,1)} %param.20), kind=kOutput, calls=%fused_computation.71 | convolution fusion | flops 1073741824 | bytes 10747904 | tf_op jit(solution)/shard_map/dot_general | solution.py:79
  17.2 0.0 reduce-scatter.4.cloned.1.call-update
  17.2 46.5 %reduce-scatter.4.cloned.1.call-done = f32[128,1024]{1,0:T(8,128)} async-done(((f32[128,4096]{1,0:T(8,128)}), f32[128,1024]{1,0:T(8,128)}) %reduce-scatter.4.cloned.1.call-update) | async-done | bytes 524304 | tf_op jit(solution)/shard_map/reduce_scatter | solution.py:80
  63.7 1.1 add_convert_fusion
  64.8 0.7 collective-permute-start
  65.6 0.1 copy.24
  65.7 0.1 reshape.92
  65.9 0.1 reshape.139
  66.0 1.4 scatter_custom_fusion
  67.4 5.1 %collective-permute-done = bf16[128,1024]{1,0:T(8,128)(2,1)S(1)} collective-permute-done((bf16[128,1024]{1,0:T(8,128)(2,1)S(1)}, bf16[128,1024]{1,0:T(8,128)(2,1)S(1)}, u32[]{:S(2)}, u32[]{:S(2)}) %collective-permute-start) | collective-permute-done | bytes 262176 | tf_op jit(solution)/shard_map/ppermute | solution.py:15
  72.5 0.1 maximum_select_fusion.1
  72.7 2.0 collective-permute-start.1
  74.8 22.5 %collective-permute-done.1 = bf16[128,2048]{1,0:T(8,128)(2,1)S(1)} collective-permute-done((bf16[128,2048]{1,0:T(8,128)(2,1)S(1)}, bf16[128,2048]{1,0:T(8,128)(2,1)S(1)}, u32[]{:S(2)}, u32[]{:S(2)}) %collective-permute-start.1) | collective-permute-done | bytes 524320 | tf_op jit(solution)/shard_map/ppermute | solution.py:15
  97.3 0.3 maximum_select_fusion
  97.5 0.1 concatenate.22
  97.6 4.4 %gather_fusion = bf16[512,4096]{1,0:T(8,128)(2,1)} fusion(bf16[129,4096]{1,0:T(8,128)(2,1)S(1)} %concatenate.22, s32[1024]{0:T(1024)S(1)} %pad_clamp_fusion.2), kind=kCustom, calls=%fused_computation.clone | custom fusion | bytes 8390656 | tf_op jit(solution)/shard_map/jit(_take)/gather | solution.py:48
  102.1 4.6 %broadcast_select_fusion = bf16[512,4096]{1,0:T(8,128)(2,1)} fusion(bf16[512,4096]{1,0:T(8,128)(2,1)} %gather_fusion, pred[512]{0:T(512)(128)(4,1)S(1)} %compare_and_fusion.2), kind=kLoop, calls=%fused_computation.16 | loop fusion | flops 2097152 | bytes 8389120 | tf_op jit(solution)/shard_map/jit(_take)/select_n | solution.py:48
  106.7 4.8 %all-to-all-start = ((bf16[4,128,4096]{2,1,0:T(8,128)(2,1)}), bf16[4,128,4096]{2,1,0:T(8,128)(2,1)}, u32[]{:S(2)}, u32[]{:S(2)}) async-start(bf16[4,128,4096]{2,1,0:T(8,128)(2,1)} %bitcast.74), calls=%async_computation.1 | async-start | bytes 8388608 | tf_op jit(solution)/shard_map/all_to_all | solution.py:106
  111.5 0.0 all-gather.2.cloned.1.call-start
  111.6 0.7 all-gather.2.cloned.1.call-update
  112.3 0.0 reduce-scatter.6.cloned.1.call-start
  112.3 47.4 %all-to-all-done = bf16[4,128,4096]{2,1,0:T(8,128)(2,1)} async-done(((bf16[4,128,4096]{2,1,0:T(8,128)(2,1)}), bf16[4,128,4096]{2,1,0:T(8,128)(2,1)}, u32[]{:S(2)}, u32[]{:S(2)}) %all-to-all-start) | async-done | bytes 4194336 | tf_op jit(solution)/shard_map/all_to_all | solution.py:106
  159.7 7.0 %fusion.5 = f32[512,800]{0,1:T(8,128)S(1)} fusion(bf16[512,4096]{1,0:T(8,128)(2,1)} %bitcast.11, bf16[1,800,4096]{2,1,0:T(8,128)(2,1)} %param.26), kind=kOutput, calls=%fused_computation.12 | convolution fusion | flops 3355443200 | bytes 12386304 | tf_op jit(solution)/shard_map/dot_general | solution.py:113
  166.7 0.0 copy-start.4
  166.7 3.6 %convolution_convert_fusion.3 = bf16[512,64]{0,1:T(8,128)(2,1)S(1)} fusion(bf16[512,4096]{1,0:T(8,128)(2,1)} %bitcast.11, bf16[1,64,4096]{2,1,0:T(8,128)(2,1)S(1)} %copy-done), kind=kOutput, calls=%fused_computation.30 | convolution fusion | flops 268468224 | bytes 4784128 | tf_op jit(solution)/shard_map/dot_general | solution.py:119
  170.4 0.4 multiply_add_fusion
  170.8 0.0 copy-start.2
  170.8 9.7 %fusion.7 = bf16[512,4096]{1,0:T(8,128)(2,1)} fusion(bf16[1,800,4096]{2,1,0:T(8,128)(2,1)} %param.27, f32[512,800]{0,1:T(8,128)S(1)} %multiply_add_fusion), kind=kOutput, calls=%fused_computation.14 | convolution fusion | flops 3359588352 | bytes 12386304 | tf_op jit(solution)/shard_map/dot_general | solution.py:130
  180.5 0.0 reduce-scatter.6.cloned.1.call-update
  180.5 0.2 reduce-scatter.8.cloned.1.call-start
  180.8 0.4 copy-done.6
  181.2 0.1 copy.25
  181.3 0.1 reshape.147
  181.4 1.4 scatter_custom_fusion.1
  182.9 0.0 all-gather.2.cloned.1.call-done
  182.9 1.3 concatenate.23
  184.2 4.4 %gather_fusion.3 = bf16[512,4096]{1,0:T(8,128)(2,1)} fusion(bf16[129,4096]{1,0:T(8,128)(2,1)S(1)} %concatenate.23, s32[1024]{0:T(1024)S(1)} %pad_clamp_fusion.2), kind=kCustom, calls=%fused_computation.2.clone | custom fusion | bytes 8390656 | tf_op jit(solution)/shard_map/jit(_take)/gather | solution.py:48
  188.6 4.6 %multiply_convert_fusion = bf16[512,4096]{1,0:T(8,128)(2,1)S(1)} fusion(bf16[512,4096]{1,0:T(8,128)(2,1)} %gather_fusion.3, f32[512]{0:T(512)S(1)} %scatter_custom_fusion.1, pred[512]{0:T(512)(128)(4,1)S(1)} %compare_and_fusion.2), kind=kLoop, calls=%fused_computation.7 | loop fusion | flops 8388608 | bytes 8391168 | tf_op jit(solution)/shard_map/convert_element_type | solution.py:52
  193.2 50.8 %all_to_all.15 = bf16[4,128,4096]{2,1,0:T(8,128)(2,1)S(1)} all-to-all(bf16[4,128,4096]{2,1,0:T(8,128)(2,1)S(1)} %bitcast.73), channel_id=1, replica_groups=mesh['group'=2,'route'=4,'cuts'=4] {'route'}, dimensions={0} | all-to-all | bytes 8388608 | tf_op jit(solution)/shard_map/all_to_all | solution.py:107
  244.0 7.0 %multiply_convert_fusion.1 = bf16[512,800]{0,1:T(8,128)(2,1)S(1)} fusion(f32[512,800]{0,1:T(8,128)S(1)} %copy-done.3, bf16[512,4096]{1,0:T(8,128)(2,1)S(1)} %bitcast.76, bf16[1,800,4096]{2,1,0:T(8,128)(2,1)} %param.27), kind=kOutput, calls=%fused_computation.17 | convolution fusion | flops 3359129600 | bytes 13205504 | tf_op jit(solution)/shard_map/dot_general | solution.py:152
  251.0 4.6 %convolution_convert_fusion = bf16[64,4096]{1,0:T(8,128)(2,1)} fusion(bf16[512,4096]{1,0:T(8,128)(2,1)} %bitcast.11, bf16[512,800]{0,1:T(8,128)(2,1)S(1)} %multiply_convert_fusion.1, bf16[1,64,800]{2,1,0:T(8,128)(2,1)S(1)} %copy-done.4), kind=kOutput, calls=%fused_computation.15 | convolution fusion | flops 321159168 | bytes 5640192 | tf_op jit(solution)/shard_map/dot_general | solution.py:167
  255.6 0.0 reduce-scatter.8.cloned.1.call-update
  255.7 0.7 reduce-scatter.6.cloned.1.call-done
  256.3 4.2 %all-to-all-start.1 = ((bf16[4,128,1024]{2,1,0:T(8,128)(2,1)}), bf16[4,128,1024]{2,1,0:T(8,128)(2,1)}, u32[]{:S(2)}, u32[]{:S(2)}) async-start(bf16[4,128,1024]{2,1,0:T(8,128)(2,1)} %reduce-scatter.6.cloned.1.call-done), calls=%async_computation.3 | async-start | bytes 2097152 | tf_op jit(solution)/shard_map/all_to_all | solution.py:142
  260.6 1.1 fusion.16
  261.7 19.1 %reduce-scatter.8.cloned.1.call-done = bf16[64,1024]{1,0:T(8,128)(2,1)} async-done(((bf16[64,4096]{1,0:T(8,128)(2,1)}), bf16[64,1024]{1,0:T(8,128)(2,1)}) %reduce-scatter.8.cloned.1.call-update) | async-done | bytes 131088 | tf_op jit(solution)/shard_map/reduce_scatter | solution.py:170
  280.8 1.6 multiply_bitcast_fusion
  282.5 0.0 all-to-all-done.1
  282.5 1.5 bitcast_convert_fusion
  283.9 0.0 copy-start.1
  283.9 0.8 gather_fusion.2
  284.7 1.6 gather_fusion.1
  286.3 2.0 fusion.21
  (20 shorter events, 0.1 us)
Async XLA Ops:
  7.2 159.6 %copy-start = (bf16[1,64,4096]{2,1,0:T(8,128)(2,1)S(1)}, bf16[1,64,4096]{2,1,0:T(8,128)(2,1)}, u32[]{:S(2)}) copy-start(bf16[1,64,4096]{2,1,0:T(8,128)(2,1)} %param.28) | copy-start | bytes 1572868
  7.2 56.6 %reduce-scatter.4.cloned.1.call-start = ((), (), s32[]{:S(2)}) async-start(), calls=%async_computation.6 | async-start | bytes 2621440 | tf_op jit(solution)/shard_map/reduce_scatter | solution.py:80
  11.1 52.6 %copy-start.5 = (bf16[128,1024]{1,0:T(8,128)(2,1)S(1)}, bf16[128,1024]{1,0:T(8,128)(2,1)}, u32[]{:S(2)}) copy-start(bf16[128,1024]{1,0:T(8,128)(2,1)} %param.21) | copy-start | bytes 786436
  11.1 54.4 %copy-start.7 = (s32[128,2]{0,1:T(2,128)S(1)}, s32[128,2]{0,1:T(2,128)}, u32[]{:S(2)}) copy-start(s32[128,2]{0,1:T(2,128)} %param.24) | copy-start | bytes 3076
  11.1 54.4 %copy-start.8 = (s32[128,2]{0,1:T(2,128)S(1)}, s32[128,2]{0,1:T(2,128)}, u32[]{:S(2)}) copy-start(s32[128,2]{0,1:T(2,128)} %param.23) | copy-start | bytes 3076
  64.8 7.7 %collective-permute-start = (bf16[128,1024]{1,0:T(8,128)(2,1)S(1)}, bf16[128,1024]{1,0:T(8,128)(2,1)S(1)}, u32[]{:S(2)}, u32[]{:S(2)}) collective-permute-start(bf16[128,1024]{1,0:T(8,128)(2,1)S(1)} %add_convert_fusion), channel_id=1, source_target_pairs={{0,1},{1,0},{2,3},{3,2},{4,5},{5,4},{6,7},{7,6},{8,9},{9,8},{10,11... | collective-permute-start | bytes 786440 | tf_op jit(solution)/shard_map/ppermute | solution.py:15
  72.7 24.6 %collective-permute-start.1 = (bf16[128,2048]{1,0:T(8,128)(2,1)S(1)}, bf16[128,2048]{1,0:T(8,128)(2,1)S(1)}, u32[]{:S(2)}, u32[]{:S(2)}) collective-permute-start(bf16[128,2048]{1,0:T(8,128)(2,1)S(1)} %maximum_select_fusion.1), channel_id=1, source_target_pairs={{0,2},{1,3},{2,0},{3,1},{4,6},{5,7},{6,4},{7,5},{8,10},{9,11},{10,... | collective-permute-start | bytes 1572872 | tf_op jit(solution)/shard_map/ppermute | solution.py:15
  106.7 53.0 %all-to-all-start = ((bf16[4,128,4096]{2,1,0:T(8,128)(2,1)}), bf16[4,128,4096]{2,1,0:T(8,128)(2,1)}, u32[]{:S(2)}, u32[]{:S(2)}) async-start(bf16[4,128,4096]{2,1,0:T(8,128)(2,1)} %bitcast.74), calls=%async_computation.1 | async-start | bytes 8388608 | tf_op jit(solution)/shard_map/all_to_all | solution.py:106
  111.5 71.4 %all-gather.2.cloned.1.call-start = ((), (), s32[]{:S(2)}) async-start(), calls=%async_computation.8 | async-start | bytes 1310720 | tf_op jit(solution)/shard_map/all_gather | solution.py:101
  112.3 144.1 %reduce-scatter.6.cloned.1.call-start = ((), (), s32[]{:S(2)}) async-start(), calls=%async_computation.7 | async-start | bytes 5242880 | tf_op jit(solution)/shard_map/reduce_scatter | solution.py:133
  166.7 3.6 %copy-start.4 = (bf16[1,64,800]{2,1,0:T(8,128)(2,1)S(1)}, bf16[1,64,800]{2,1,0:T(8,128)(2,1)}, u32[]{:S(2)}) copy-start(bf16[1,64,800]{2,1,0:T(8,128)(2,1)} %param.29) | copy-start | bytes 307204
  170.8 9.7 %copy-start.2 = (f32[512,800]{0,1:T(8,128)}, f32[512,800]{0,1:T(8,128)S(1)}, u32[]{:S(2)}) copy-start(f32[512,800]{0,1:T(8,128)S(1)} %multiply_add_fusion) | copy-start | bytes 4915204
  180.5 0.7 copy-start.6
  180.5 100.3 %reduce-scatter.8.cloned.1.call-start = ((), (), s32[]{:S(2)}) async-start(), calls=%async_computation.9 | async-start | bytes 655360 | tf_op jit(solution)/shard_map/reduce_scatter | solution.py:170
  193.2 50.8 %copy-start.3 = (f32[512,800]{0,1:T(8,128)S(1)}, f32[512,800]{0,1:T(8,128)}, u32[]{:S(2)}) copy-start(f32[512,800]{0,1:T(8,128)} %copy-done.2) | copy-start | bytes 4915204
  256.3 26.1 %all-to-all-start.1 = ((bf16[4,128,1024]{2,1,0:T(8,128)(2,1)}), bf16[4,128,1024]{2,1,0:T(8,128)(2,1)}, u32[]{:S(2)}, u32[]{:S(2)}) async-start(bf16[4,128,1024]{2,1,0:T(8,128)(2,1)} %reduce-scatter.6.cloned.1.call-done), calls=%async_computation.3 | async-start | bytes 2097152 | tf_op jit(solution)/shard_map/all_to_all | solution.py:142
  283.9 4.4 %copy-start.1 = (bf16[1,64,4096]{2,1,0:T(8,128)(2,1)S(1)}, bf16[1,64,4096]{2,1,0:T(8,128)(2,1)}, u32[]{:S(2)}) copy-start(bf16[1,64,4096]{2,1,0:T(8,128)(2,1)} %param.28) | copy-start | bytes 1572868
Sparse Core Ops, SparseCore 0:
  17.4 46.3 reduce-scatter.3
  113.9 28.2 all-gather.1
  180.7 75.6 reduce-scatter.5
  258.5 22.3 reduce-scatter.7
